TPU v7x, 32 devices: a whole 2x2x4 slice. The times are simulated.
32 devices in a mesh: lat: 4 (over x, core), lon: 8 (over z, y).
Axes of the slice: x: 2, y: 2, z: 4, core: 2. Of those that a mesh axis runs over, the one named last changes fastest.
Arguments:
- tokens: bfloat16 [32, 1440, 512], P('lat', 'lon'), may hold values from -6 to 6
- ln_gain: float32 [512], replicated, may hold values from 0.25 to 1.75
- w_qkv: bfloat16 [512, 1536], replicated, may hold values from -6 to 6
- w_out: bfloat16 [512, 512], replicated, may hold values from -1 to 1
- zonal_slope: float32 [4], replicated, may hold values from 0.5 to 8
- merid_slope: float32 [4], replicated, may hold values from 0.5 to 8
Outputs:
- update: bfloat16 [32, 1440, 512], P('lat', 'lon')
All inputs are finite; a program needn't handle non-finite values.
Results may differ from a plain program's by a relative error of at most 0.0084.
Values may be sent and summed in bfloat16 or wider, within the bound.
A program may use at most 128 MiB of HBM per device.

v0:
```python
import functools
import math
import jax
import jax.numpy as jnp
from jax import lax
from jax.experimental import pallas as pl
from jax.experimental.pallas import tpu as pltpu
from jax.sharding import PartitionSpec as P

HEADS = 8
HD = 64
HALF = HEADS // 2
GW = HALF * HD
LOG2E = math.log2(math.e)
FAR = -1e30
BF = jnp.bfloat16
F32 = jnp.float32
MESH = pl.DeviceIdType.MESH

def norm_rows(tokens, gain):
    values = tokens.astype(jnp.float32)
    center = values - jnp.mean(values, axis=-1, keepdims=True)
    spread = jnp.mean(center * center, axis=-1, keepdims=True)
    return (center * lax.rsqrt(spread + 1e-05) * gain).astype(jnp.bfloat16)


def fold_step(carry, scores, values, form):
    top, total, summed = carry
    top_new = jnp.maximum(top, jnp.max(scores, axis=-1))
    weights = jnp.exp(scores - top_new[..., None])
    total = jnp.sum(weights, axis=-1)
    summed = jnp.einsum(
        form, weights.astype(jnp.bfloat16), values, preferred_element_type=jnp.float32
    )
    return (top_new, total, summed)


def gathered(tokens, ln_gain, w_qkv, w_out, zonal_slope, merid_slope):
    lat_rows, lon_cols, width = tokens.shape
    half = HEADS // 2
    scale = HD ** (-0.5)
    normed = norm_rows(tokens, ln_gain)
    qkv = jnp.dot(
        normed.reshape(lat_rows * lon_cols, width), w_qkv, preferred_element_type=jnp.float32
    ).astype(jnp.bfloat16)
    qkv = qkv.reshape(lat_rows, lon_cols, 3, 2, half, HD)
    lon_total = lon_cols * lax.axis_size("lon")
    lat_total = lat_rows * lax.axis_size("lat")
    zonal_query = qkv[:, :, 0, 0]
    zonal_pairs = qkv[:, :, 1:, 0]
    query_pos = lax.axis_index("lon") * lon_cols + jnp.arange(lon_cols, dtype=jnp.int32)
    start_carry = (
        jnp.full((lat_rows, half, lon_cols), -1e30, jnp.float32),
        jnp.zeros((lat_rows, half, lon_cols), jnp.float32),
        jnp.zeros((lat_rows, half, lon_cols, HD), jnp.float32),
    )
    piece = lax.all_gather(zonal_pairs, "lon", axis=1, tiled=True)
    count = piece.shape[1]
    key_pos = jnp.arange(count, dtype=jnp.int32)
    gap = jnp.abs(query_pos[:, None] - key_pos[None, :])
    circle = jnp.minimum(gap, lon_total - gap).astype(jnp.float32) / lon_total
    bias = -zonal_slope[:, None, None] * circle[None]
    scores = (
        jnp.einsum(
            "ajhd,akhd->ahjk", zonal_query, piece[:, :, 0], preferred_element_type=jnp.float32
        )
        * scale
        + bias[None]
    )
    top, total, summed = fold_step(start_carry, scores, piece[:, :, 1], "ahjk,akhd->ahjd")
    zonal = jnp.transpose(summed / total[..., None], (0, 2, 1, 3)).reshape(
        lat_rows, lon_cols, half * HD
    )
    merid_query = qkv[:, :, 0, 1]
    merid_pairs = qkv[:, :, 1:, 1]
    row_pos = lax.axis_index("lat") * lat_rows + jnp.arange(lat_rows, dtype=jnp.int32)
    start_carry = (
        jnp.full((lon_cols, half, lat_rows), -1e30, jnp.float32),
        jnp.zeros((lon_cols, half, lat_rows), jnp.float32),
        jnp.zeros((lon_cols, half, lat_rows, HD), jnp.float32),
    )
    piece = lax.all_gather(merid_pairs, "lat", axis=0, tiled=True)
    count = piece.shape[0]
    key_pos = jnp.arange(count, dtype=jnp.int32)
    gap = jnp.abs(row_pos[:, None] - key_pos[None, :]).astype(jnp.float32) / lat_total
    bias = -merid_slope[:, None, None] * gap[None]
    scores = (
        jnp.einsum(
            "ajhd,bjhd->jhab", merid_query, piece[:, :, 0], preferred_element_type=jnp.float32
        )
        * scale
        + bias[None]
    )
    top, total, summed = fold_step(start_carry, scores, piece[:, :, 1], "jhab,bjhd->jhad")
    merid = jnp.transpose(summed / total[..., None], (2, 0, 1, 3)).reshape(
        lat_rows, lon_cols, half * HD
    )
    attended = jnp.concatenate([zonal, merid], axis=-1).astype(jnp.bfloat16)
    update = jnp.dot(
        attended.reshape(lat_rows * lon_cols, width), w_out, preferred_element_type=jnp.float32
    )
    return update.astype(jnp.bfloat16).reshape(lat_rows, lon_cols, width)

def normed_of(x, gain):
    v = x.astype(F32)
    c = v - jnp.mean(v, axis=-1, keepdims=True)
    s = jnp.mean(c * c, axis=-1, keepdims=True)
    return (c * lax.rsqrt(s + 1e-05) * gain).astype(BF)


def mm(a, b):
    return jnp.dot(a, b, preferred_element_type=F32)


def mm_t(a, b):
    return lax.dot_general(a, b, (((1,), (1,)), ((), ())), preferred_element_type=F32)


def split_query(acc):
    q = acc.astype(BF).astype(F32) * (HD ** (-0.5) * LOG2E)
    hi = q.astype(BF).astype(F32)
    return hi, q - hi


def kernel(dims, tok_ref, gain_ref, wqkv_ref, zs_ref, ms_ref, out_ref,
           flat, rowsrc, rowbuf, colbuf, qx, kx, vx, zbias, mbias, mqkv, s_ref, p_ref, o_ref,
           zout, mout, zret, mret, zflat,
           zsend, zrecv, msend, mrecv, zrs, zrr, mrs, mrr):
    nlon, nlat, rows, cols, width = dims
    chunk = cols // nlat
    step = qx.shape[1] // nlon
    qb = 2 * step
    nblk = nlon // 2
    half = nblk // 2
    span = nlon * step
    lon_total = nlon * cols
    lat_total = nlat * rows
    me = lax.axis_index("lon")
    la = lax.axis_index("lat")

    barrier = pltpu.get_barrier_semaphore()
    for k in range(1, nlon):
        pl.semaphore_signal(barrier, inc=1, device_id={"lon": lax.rem(me + k, nlon)}, device_id_type=MESH)
    for k in range(1, nlat):
        pl.semaphore_signal(barrier, inc=1, device_id={"lat": lax.rem(la + k, nlat)}, device_id_type=MESH)
    pl.semaphore_wait(barrier, nlon + nlat - 2)

    def zcopy(dst, src):
        return pltpu.make_async_remote_copy(
            src_ref=rowsrc.at[dst], dst_ref=rowbuf.at[src], send_sem=zsend.at[dst],
            recv_sem=zrecv.at[src], device_id={"lon": dst}, device_id_type=MESH)

    def mcopy(dst, src):
        return pltpu.make_async_remote_copy(
            src_ref=tok_ref.at[pl.ds(dst * chunk, chunk)],
            dst_ref=colbuf.at[src], send_sem=msend.at[dst],
            recv_sem=mrecv.at[src], device_id={"lat": dst}, device_id_type=MESH)

    def zback(dst, src):
        return pltpu.make_async_remote_copy(
            src_ref=zout.at[dst], dst_ref=zret.at[src], send_sem=zrs.at[dst],
            recv_sem=zrr.at[src], device_id={"lon": dst}, device_id_type=MESH)

    def mback(dst, src):
        return pltpu.make_async_remote_copy(
            src_ref=mout.at[dst],
            dst_ref=mret.at[pl.ds(src * chunk, chunk)], send_sem=mrs.at[dst],
            recv_sem=mrr.at[src], device_id={"lat": dst}, device_id_type=MESH)

    for k in range(1, nlat):
        mcopy(lax.rem(la + k, nlat), la).start()

    def flatten(i, _):
        part = tok_ref[pl.ds(i * chunk, chunk)].astype(F32).reshape(chunk * rows, width)
        for j in range(width // 128):
            flat[j, pl.ds(pl.multiple_of(i * chunk * rows, 8), chunk * rows), :] = part[:, j * 128:j * 128 + 128]
        return 0

    lax.fori_loop(0, nlat, flatten, 0)

    def take_row(r):
        for j in range(width // 128):
            rowsrc[r, :, j * 128:j * 128 + 128] = flat[j, pl.ds(r, cols, stride=rows), :].astype(BF)

    far_first = sorted(range(1, nlon), key=lambda k: -min(k, nlon - k))
    for k in far_first:
        r = lax.rem(me + k, nlon)
        take_row(r)
        zcopy(r, me).start()
    take_row(me)

    kx[...] = jnp.zeros_like(kx)
    vx[...] = jnp.zeros_like(vx)
    qx[...] = jnp.zeros_like(qx)
    gain = gain_ref[...]

    def zbias_stripe(i, _):
        r = i * 32 + lax.broadcasted_iota(jnp.int32, (32, 1), 0)
        c = lax.broadcasted_iota(jnp.int32, (1, span), 1)
        cc = c // step
        cj = c - cc * step
        rc = r // step
        gap = jnp.abs((rc * cols + (r - rc * step)) - (cc * cols + cj))
        circle = jnp.minimum(gap, lon_total - gap).astype(F32) * (LOG2E / lon_total)
        dead = cj >= cols
        for h in range(HALF):
            zbias[h, pl.ds(pl.multiple_of(i * 32, 32), 32), :] = jnp.where(dead, FAR, -zs_ref[h] * circle)
        return 0

    lax.fori_loop(0, qb // 32, zbias_stripe, 0)
    group = mbias.shape[1]
    mr = lax.broadcasted_iota(jnp.int32, (group, 1), 0)
    mc = lax.broadcasted_iota(jnp.int32, (1, group), 1)
    mgap = jnp.abs(mr % lat_total - mc % lat_total).astype(F32) * (LOG2E / lat_total)
    for h in range(HALF):
        mbias[h] = jnp.where(mr // lat_total == mc // lat_total, -ms_ref[h] * mgap, FAR)

    def project_zonal(x, p):
        n = normed_of(x, gain)
        hi, lo = split_query(mm(n, wqkv_ref[:, 0:GW]))
        k = mm(n, wqkv_ref[:, 2 * GW:3 * GW])
        v = mm(n, wqkv_ref[:, 4 * GW:5 * GW])
        one = jnp.ones((cols, HD), F32)
        at = pl.ds(pl.multiple_of(p * step, 16), cols)
        for h in range(HALF):
            w = slice(h * HD, h * HD + HD)
            qx[h, at, :] = jnp.concatenate([hi[:, w], lo[:, w]], axis=1).astype(BF)
            kh = jnp.concatenate([k[:, w], k[:, w]], axis=1).astype(BF)
            vh = jnp.concatenate([v[:, w], one], axis=1).astype(BF)
            again = pl.ds(pl.multiple_of(p * step + span, 16), cols)
            kx[h, at, :] = kh
            kx[h, again, :] = kh
            vx[h, at, :] = vh
            vx[h, again, :] = vh

    def project_merid(x, a):
        n = normed_of(x, gain).reshape(chunk * rows, width)
        at = pl.ds(pl.multiple_of(a * rows, 8), rows)
        for i in range(3):
            mqkv[i, :, at, :] = mm(n, wqkv_ref[:, (2 * i + 1) * GW:(2 * i + 2) * GW]).reshape(chunk, rows, GW)

    project_zonal(rowsrc[me], me)
    project_merid(tok_ref[pl.ds(la * chunk, chunk)], la)

    def more_merid(k, _):
        a = lax.rem(la + k, nlat)
        mcopy(la, a).wait_recv()
        project_merid(colbuf[a], a)
        return 0

    lax.fori_loop(1, nlat, more_merid, 0)

    gcols = group // lat_total

    def merid_group(g, _):
        at = pl.ds(g * gcols, gcols)
        hi, lo = split_query(mqkv[0, at].reshape(group, GW))
        k = mqkv[1, at].reshape(group, GW)
        v = mqkv[2, at].reshape(group, GW)
        one = jnp.ones((group, HD), F32)
        outs = []
        for h in range(HALF):
            w = slice(h * HD, h * HD + HD)
            qh = jnp.concatenate([hi[:, w], lo[:, w]], axis=1).astype(BF)
            kh = jnp.concatenate([k[:, w], k[:, w]], axis=1).astype(BF)
            vh = jnp.concatenate([v[:, w], one], axis=1).astype(BF)
            s = mm_t(qh, kh) + mbias[h]
            e = jnp.exp2(s - jnp.max(s, axis=-1, keepdims=True)).astype(BF)
            o = mm(e, vh)
            outs.append(o[:, :HD] / o[:, HD:])
        o = jnp.concatenate(outs, axis=1).reshape(gcols, lat_total, GW)
        for a in range(nlat):
            mout[a, at] = o[:, a * rows:(a + 1) * rows, :].astype(BF)
        return 0

    lax.fori_loop(0, chunk // gcols, merid_group, 0, unroll=3 if chunk // gcols % 3 == 0 else 1)
    for k in range(1, nlat):
        mback(lax.rem(la + k, nlat), la).start()
    mret[pl.ds(la * chunk, chunk)] = mout[la]

    my_blk = me // 2
    my_half = my_blk // half

    def more_zonal(i, _):
        t = i // 2
        blk = lax.rem(my_half + t // half, 2) * half + lax.rem(my_blk + t, half)
        p = blk * 2 + lax.rem(me + i, 2)
        zcopy(me, p).wait_recv()
        project_zonal(rowbuf[p], p)
        return 0

    lax.fori_loop(1, nlon, more_zonal, 0)

    def far_block(t):
        return lax.rem(my_half + 1 + t // half, 2) * half + lax.rem(my_blk + t + t // half, half)

    def zonal_block(t, _):
        blk = far_block(t)
        qat = pl.ds(pl.multiple_of(blk * qb, 16), qb)
        kat = pl.ds(pl.multiple_of(blk * qb, 16), span)
        for h in range(HALF):
            slot = h % 2
            s_ref[slot] = mm_t(qx[h, qat, :], kx[h, kat, :]) + zbias[h]
            for i in range(qb // 32):
                at = slice(i * 32, i * 32 + 32)
                s = s_ref[slot, at, :]
                p_ref[slot, at, :] = jnp.exp2(s - jnp.max(s, axis=-1, keepdims=True)).astype(BF)
            o_ref[h] = mm(p_ref[slot], vx[h, kat, :])
        outs = [o_ref[h, :, :HD] / o_ref[h, :, HD:] for h in range(HALF)]
        o = jnp.concatenate(outs, axis=1).astype(BF)
        for u in range(2):
            dst = blk * 2 + u
            zout[dst] = o[u * step:u * step + cols]

            @pl.when(dst != me)
            def _():
                zback(dst, me).start()
        return 0

    lax.fori_loop(0, nblk, zonal_block, 0)
    zret[me] = zout[me]

    for k in range(1, nlat):
        mback(la, lax.rem(la + k, nlat)).wait_recv()
    out_ref[:, :, GW:2 * GW] = mret[...]

    def finish(i, _):
        s = far_block(i // 2) * 2 + lax.rem(i, 2)

        @pl.when(s != me)
        def _():
            zback(me, s).wait_recv()

        for j in range(GW // 128):
            zflat[j, pl.ds(s, cols, stride=rows), :] = zret[s, :, j * 128:j * 128 + 128].astype(F32)
        return 0

    lax.fori_loop(0, nlon, finish, 0)
    for j in range(GW // 128):
        out_ref[:, :, j * 128:j * 128 + 128] = zflat[j].reshape(cols, rows, 128).astype(BF)

    for k in range(1, nlon):
        p = lax.rem(me + k, nlon)
        zcopy(p, me).wait_send()
        zback(p, me).wait_send()
    for k in range(1, nlat):
        a = lax.rem(la + k, nlat)
        mcopy(a, la).wait_send()
        mback(a, la).wait_send()


def up(n, m):
    return -(-n // m) * m


def exchanged(nlon, nlat, tokens, ln_gain, w_qkv, w_out, zonal_slope, merid_slope):
    rows, cols, width = tokens.shape
    chunk = cols // nlat
    step = up(cols, 64)
    span = nlon * step
    lat_total = nlat * rows
    gcols = max(d for d in range(1, 128 // lat_total + 1) if chunk % d == 0)
    group = gcols * lat_total
    qb = 2 * step
    vm = pl.BlockSpec(memory_space=pltpu.VMEM)
    sm = pl.BlockSpec(memory_space=pltpu.SMEM)
    dma = pltpu.SemaphoreType.DMA
    attended = pl.pallas_call(
        functools.partial(kernel, (nlon, nlat, rows, cols, width)),
        out_shape=jax.ShapeDtypeStruct((cols, rows, width), BF),
        in_specs=[vm, vm, vm, sm, sm],
        out_specs=vm,
        scratch_shapes=[
            pltpu.VMEM((width // 128, cols * rows, 128), F32),
            pltpu.VMEM((nlon, cols, width), BF),
            pltpu.VMEM((nlon, cols, width), BF),
            pltpu.VMEM((nlat, chunk, rows, width), BF),
            pltpu.VMEM((HALF, span, 2 * HD), BF),
            pltpu.VMEM((HALF, 2 * span, 2 * HD), BF),
            pltpu.VMEM((HALF, 2 * span, 2 * HD), BF),
            pltpu.VMEM((HALF, qb, span), F32),
            pltpu.VMEM((HALF, group, group), F32),
            pltpu.VMEM((3, chunk, lat_total, GW), F32),
            pltpu.VMEM((2, qb, span), F32),
            pltpu.VMEM((2, qb, span), BF),
            pltpu.VMEM((HALF, qb, 2 * HD), F32),
            pltpu.VMEM((nlon, cols, GW), BF),
            pltpu.VMEM((nlat, chunk, rows, GW), BF),
            pltpu.VMEM((nlon, cols, GW), BF),
            pltpu.VMEM((cols, rows, GW), BF),
            pltpu.VMEM((GW // 128, cols * rows, 128), F32),
            dma((nlon,)), dma((nlon,)), dma((nlat,)), dma((nlat,)),
            dma((nlon,)), dma((nlon,)), dma((nlat,)), dma((nlat,)),
        ],
        compiler_params=pltpu.CompilerParams(
            collective_id=0, has_side_effects=True, vmem_limit_bytes=62 * 1024 * 1024),
        name="axial",
    )(jnp.transpose(tokens, (1, 0, 2)), ln_gain.reshape(1, width), w_qkv, zonal_slope, merid_slope)
    update = mm(attended.reshape(cols * rows, width), w_out).astype(BF)
    return jnp.transpose(update.reshape(cols, rows, width), (1, 0, 2))


def solution(mesh):
    nlon, nlat = mesh.shape["lon"], mesh.shape["lat"]

    def body(tokens, *rest):
        rows, cols, _ = tokens.shape
        if rows == 8 == nlon and cols % nlat == 0 and nlat * rows <= 64:
            return exchanged(nlon, nlat, tokens, *rest)
        return gathered(tokens, *rest)

    return jax.shard_map(
        body, mesh=mesh, in_specs=(P("lat", "lon", None), P(), P(), P(), P(), P()),
        out_specs=P("lat", "lon", None), check_vma=False
    )
```

profile of v0, /device:TPU:1, one launch (start us, length us, event | category | flops | bytes accessed | tf_op | source)
XLA Modules:
  0.0 70.9 jit_solution(554300956407465296)
XLA Ops:
  0.0 0.0 copy-start
  0.0 67.5 %axial.1 = bf16[180,8,512]{2,1,0:T(8,128)(2,1)} custom-call(bf16[180,8,512]{2,1,0:T(8,128)(2,1)} %bitcast.12, f32[1,512]{1,0:T(1,128)} %bitcast.13, bf16[512,1536]{1,0:T(8,128)(2,1)} %wqkv_ref.1, f32[4]{0:T(128)} %zs_ref.1, f32[4]{0:T(128)} %ms_ref.1), custom_call_target="tpu_custom_call" | custom-call | tf_op jit(solution)/shard_map/axial/pallas_call | solution.py:368
  67.5 0.0 copy-done
  67.5 3.4 %fusion.1 = bf16[8,180,512]{2,0,1:T(8,128)(2,1)} fusion(bf16[512,512]{1,0:T(8,128)(2,1)S(1)} %copy-done, bf16[180,8,512]{2,1,0:T(8,128)(2,1)} %axial.1), kind=kOutput, calls=%fused_computation.2 | convolution fusion | flops 755712000 | bytes 3473408 | tf_op jit(solution)/shard_map/dot_general | solution.py:112
Async XLA Ops:
  0.0 67.5 %copy-start = (bf16[512,512]{1,0:T(8,128)(2,1)S(1)}, bf16[512,512]{1,0:T(8,128)(2,1)}, u32[]{:S(2)}) copy-start(bf16[512,512]{1,0:T(8,128)(2,1)} %param.9) | copy-start | bytes 1572868
where the time goes:
time: 71.1 us; the launch traced here: 70.9 us
  Pallas kernels  67.5 us (95%)
  matrix products  3.41 us (5%)
    pallas_call x1, Pallas kernels, exchanged(): pl.pallas_call(functools.partial(kernel, (nlon, nlat, rows, cols, width))...  67.5 us
    dot_general x1, matrix products, mm(): return jnp.dot(a, b, preferred_element_type=F32)  3.41 us

commit v1 on v0

--- a/solution.py
+++ b/solution.py
@@ -116,27 +116,37 @@
     return lax.dot_general(a, b, (((1,), (1,)), ((), ())), preferred_element_type=F32)
 
 
-def split_query(acc):
-    q = acc.astype(BF).astype(F32) * (HD ** (-0.5) * LOG2E)
-    hi = q.astype(BF).astype(F32)
-    return hi, q - hi
+def batch_of(n):
+    return max(d for d in range(1, 6) if n % d == 0)
 
 
 def kernel(dims, tok_ref, gain_ref, wqkv_ref, zs_ref, ms_ref, out_ref,
            flat, rowsrc, rowbuf, colbuf, qx, kx, vx, zbias, mbias, mqkv, s_ref, p_ref, o_ref,
+           m_ref, al_ref, lt_ref, acc, den, ms_scr, mp_scr, ml_scr,
            zout, mout, zret, mret, zflat,
            zsend, zrecv, msend, mrecv, zrs, zrr, mrs, mrr):
     nlon, nlat, rows, cols, width = dims
     chunk = cols // nlat
     step = qx.shape[1] // nlon
     qb = 2 * step
-    nblk = nlon // 2
-    half = nblk // 2
     span = nlon * step
     lon_total = nlon * cols
     lat_total = nlat * rows
+    pairs = HALF // 2
     me = lax.axis_index("lon")
     la = lax.axis_index("lat")
+    zi = me // 2
+    yi = lax.rem(me, 2)
+    odd = lax.rem(zi + yi, 2)
+
+    def bit(a, b):
+        return a + b - 2 * a * b
+
+    def block_of(slot):
+        return 2 * bit(zi // 2, slot // 2) + bit(lax.rem(zi, 2), slot % 2)
+
+    def peer(slot, flip):
+        return 2 * block_of(slot) + bit(yi, flip)
 
     barrier = pltpu.get_barrier_semaphore()
     for k in range(1, nlon):
@@ -178,20 +188,26 @@
 
     lax.fori_loop(0, nlat, flatten, 0)
 
-    def take_row(r):
+    def take_row(r, to):
         for j in range(width // 128):
-            rowsrc[r, :, j * 128:j * 128 + 128] = flat[j, pl.ds(r, cols, stride=rows), :].astype(BF)
-
-    far_first = sorted(range(1, nlon), key=lambda k: -min(k, nlon - k))
-    for k in far_first:
-        r = lax.rem(me + k, nlon)
-        take_row(r)
+            to[r, :, j * 128:j * 128 + 128] = flat[j, pl.ds(r, cols, stride=rows), :].astype(BF)
+
+    same = ((1, 1), (2, 0), (3, 1))
+    other = ((0, 1), (1, 0), (2, 1), (3, 0))
+    for a, b in zip(same + other, other + same):
+        r = (1 - odd) * peer(*a) + odd * peer(*b)
+        take_row(r, rowsrc)
         zcopy(r, me).start()
-    take_row(me)
-
-    kx[...] = jnp.zeros_like(kx)
-    vx[...] = jnp.zeros_like(vx)
-    qx[...] = jnp.zeros_like(qx)
+    take_row(me, rowbuf)
+
+    edge = step - step % 16 - 16
+    for p in range(nlon):
+        at = pl.ds(p * step + edge, 16)
+        for h in range(HALF):
+            qx[h, at, :] = jnp.zeros((16, 2 * HD), BF)
+        for h in range(pairs):
+            kx[h, at, :] = jnp.zeros((16, 2 * HD), BF)
+            vx[h, at, :] = jnp.zeros((16, 2 * HD), BF)
     gain = gain_ref[...]
 
     def zbias_stripe(i, _):
@@ -201,37 +217,40 @@
         cj = c - cc * step
         rc = r // step
         gap = jnp.abs((rc * cols + (r - rc * step)) - (cc * cols + cj))
-        circle = jnp.minimum(gap, lon_total - gap).astype(F32) * (LOG2E / lon_total)
+        circle = jnp.minimum(gap, lon_total - gap).astype(F32) * (1.0 / lon_total)
         dead = cj >= cols
         for h in range(HALF):
             zbias[h, pl.ds(pl.multiple_of(i * 32, 32), 32), :] = jnp.where(dead, FAR, -zs_ref[h] * circle)
         return 0
 
     lax.fori_loop(0, qb // 32, zbias_stripe, 0)
-    group = mbias.shape[1]
+    group = mbias.shape[2]
     mr = lax.broadcasted_iota(jnp.int32, (group, 1), 0)
     mc = lax.broadcasted_iota(jnp.int32, (1, group), 1)
-    mgap = jnp.abs(mr % lat_total - mc % lat_total).astype(F32) * (LOG2E / lat_total)
+    mgap = jnp.abs(mr % lat_total - mc % lat_total).astype(F32) * (1.0 / lat_total)
     for h in range(HALF):
-        mbias[h] = jnp.where(mr // lat_total == mc // lat_total, -ms_ref[h] * mgap, FAR)
-
-    def project_zonal(x, p):
+        mbias[h // 2, h % 2 * group:(h % 2 + 1) * group] = jnp.where(
+            mr // lat_total == mc // lat_total, -ms_ref[h] * mgap, FAR)
+
+    def low(n):
+        return lax.broadcasted_iota(jnp.int32, (n, 2 * HD), 1) < HD
+
+    def split_heads(q):
+        q = q.astype(BF).astype(F32) * HD ** (-0.5)
+        keep = low(q.shape[0])
+        return jnp.where(keep, q, 0.0).astype(BF), jnp.where(keep, 0.0, q).astype(BF)
+
+    def project_zonal(x, row):
         n = normed_of(x, gain)
-        hi, lo = split_query(mm(n, wqkv_ref[:, 0:GW]))
+        q = mm(n, wqkv_ref[:, 0:GW])
         k = mm(n, wqkv_ref[:, 2 * GW:3 * GW])
         v = mm(n, wqkv_ref[:, 4 * GW:5 * GW])
-        one = jnp.ones((cols, HD), F32)
-        at = pl.ds(pl.multiple_of(p * step, 16), cols)
-        for h in range(HALF):
-            w = slice(h * HD, h * HD + HD)
-            qx[h, at, :] = jnp.concatenate([hi[:, w], lo[:, w]], axis=1).astype(BF)
-            kh = jnp.concatenate([k[:, w], k[:, w]], axis=1).astype(BF)
-            vh = jnp.concatenate([v[:, w], one], axis=1).astype(BF)
-            again = pl.ds(pl.multiple_of(p * step + span, 16), cols)
-            kx[h, at, :] = kh
-            kx[h, again, :] = kh
-            vx[h, at, :] = vh
-            vx[h, again, :] = vh
+        at = pl.ds(pl.multiple_of(row, 64), cols)
+        for h in range(pairs):
+            w = slice(h * 2 * HD, (h + 1) * 2 * HD)
+            qx[2 * h, at, :], qx[2 * h + 1, at, :] = split_heads(q[:, w])
+            kx[h, at, :] = k[:, w].astype(BF)
+            vx[h, at, :] = v[:, w].astype(BF)
 
     def project_merid(x, a):
         n = normed_of(x, gain).reshape(chunk * rows, width)
@@ -239,85 +258,162 @@
         for i in range(3):
             mqkv[i, :, at, :] = mm(n, wqkv_ref[:, (2 * i + 1) * GW:(2 * i + 2) * GW]).reshape(chunk, rows, GW)
 
-    project_zonal(rowsrc[me], me)
-    project_merid(tok_ref[pl.ds(la * chunk, chunk)], la)
-
-    def more_merid(k, _):
-        a = lax.rem(la + k, nlat)
-        mcopy(la, a).wait_recv()
-        project_merid(colbuf[a], a)
-        return 0
-
-    lax.fori_loop(1, nlat, more_merid, 0)
-
-    gcols = group // lat_total
-
-    def merid_group(g, _):
-        at = pl.ds(g * gcols, gcols)
-        hi, lo = split_query(mqkv[0, at].reshape(group, GW))
-        k = mqkv[1, at].reshape(group, GW)
-        v = mqkv[2, at].reshape(group, GW)
-        one = jnp.ones((group, HD), F32)
-        outs = []
-        for h in range(HALF):
-            w = slice(h * HD, h * HD + HD)
-            qh = jnp.concatenate([hi[:, w], lo[:, w]], axis=1).astype(BF)
-            kh = jnp.concatenate([k[:, w], k[:, w]], axis=1).astype(BF)
-            vh = jnp.concatenate([v[:, w], one], axis=1).astype(BF)
-            s = mm_t(qh, kh) + mbias[h]
-            e = jnp.exp2(s - jnp.max(s, axis=-1, keepdims=True)).astype(BF)
-            o = mm(e, vh)
-            outs.append(o[:, :HD] / o[:, HD:])
-        o = jnp.concatenate(outs, axis=1).reshape(gcols, lat_total, GW)
-        for a in range(nlat):
-            mout[a, at] = o[:, a * rows:(a + 1) * rows, :].astype(BF)
-        return 0
-
-    lax.fori_loop(0, chunk // gcols, merid_group, 0, unroll=3 if chunk // gcols % 3 == 0 else 1)
-    for k in range(1, nlat):
-        mback(lax.rem(la + k, nlat), la).start()
-    mret[pl.ds(la * chunk, chunk)] = mout[la]
-
-    my_blk = me // 2
-    my_half = my_blk // half
-
-    def more_zonal(i, _):
-        t = i // 2
-        blk = lax.rem(my_half + t // half, 2) * half + lax.rem(my_blk + t, half)
-        p = blk * 2 + lax.rem(me + i, 2)
-        zcopy(me, p).wait_recv()
-        project_zonal(rowbuf[p], p)
-        return 0
-
-    lax.fori_loop(1, nlon, more_zonal, 0)
-
-    def far_block(t):
-        return lax.rem(my_half + 1 + t // half, 2) * half + lax.rem(my_blk + t + t // half, half)
-
-    def zonal_block(t, _):
-        blk = far_block(t)
-        qat = pl.ds(pl.multiple_of(blk * qb, 16), qb)
-        kat = pl.ds(pl.multiple_of(blk * qb, 16), span)
+    def take_pieces(first, count):
+        def one(i, _):
+            slot = i // 2
+            p = peer(slot, i % 2)
+
+            @pl.when(p != me)
+            def _():
+                zcopy(me, p).wait_recv()
+
+            project_zonal(rowbuf[p], slot * qb + lax.rem(p, 2) * step)
+            return 0
+
+        lax.fori_loop(first, first + count, one, 0)
+
+    def attend(a, b0, nk, fresh):
+        qat = pl.ds(pl.multiple_of(a * qb, 128), qb)
+        kat = pl.ds(b0 * qb, nk * qb)
+        wide = nk * qb
+        turn = [lax.rem(block_of(b0 + i) - block_of(a) + 4, 4) * qb for i in range(nk)]
         for h in range(HALF):
             slot = h % 2
-            s_ref[slot] = mm_t(qx[h, qat, :], kx[h, kat, :]) + zbias[h]
+            pr = h // 2
+            s = mm_t(qx[h, qat, :], kx[pr, kat, :])
+            for i in range(nk):
+                s_ref[slot, :, i * qb:(i + 1) * qb] = (
+                    s[:, i * qb:(i + 1) * qb] + zbias[h, :, pl.ds(pl.multiple_of(turn[i], 128), qb)])
             for i in range(qb // 32):
                 at = slice(i * 32, i * 32 + 32)
-                s = s_ref[slot, at, :]
-                p_ref[slot, at, :] = jnp.exp2(s - jnp.max(s, axis=-1, keepdims=True)).astype(BF)
-            o_ref[h] = mm(p_ref[slot], vx[h, kat, :])
-        outs = [o_ref[h, :, :HD] / o_ref[h, :, HD:] for h in range(HALF)]
-        o = jnp.concatenate(outs, axis=1).astype(BF)
+                s = s_ref[slot, at, :wide]
+                top = jnp.max(s, axis=-1, keepdims=True)
+                top = jnp.broadcast_to(top, (32, 2 * HD))
+                if not fresh:
+                    before = m_ref[a, h, at, :]
+                    top = jnp.maximum(top, before)
+                    al_ref[h, at, :] = jnp.exp2((before - top) * LOG2E)
+                m_ref[a, h, at, :] = top
+                e = jnp.exp2((s - jnp.concatenate([top] * (wide // (2 * HD)), axis=1)) * LOG2E)
+                lt_ref[h, at, :] = jnp.broadcast_to(jnp.sum(e, axis=-1, keepdims=True), (32, 2 * HD))
+                p_ref[slot, at, :wide] = e.astype(BF)
+            o_ref[h] = mm(p_ref[slot, :, :wide], vx[pr, kat, :])
+        keep = low(qb)
+        for pr in range(pairs):
+            o = jnp.where(keep, o_ref[2 * pr], o_ref[2 * pr + 1])
+            d = jnp.where(keep, lt_ref[2 * pr], lt_ref[2 * pr + 1])
+            if not fresh:
+                al = jnp.where(keep, al_ref[2 * pr], al_ref[2 * pr + 1])
+                o = o + acc[a, pr] * al
+                d = d + den[a, pr] * al
+            acc[a, pr] = o
+            den[a, pr] = d
+
+    def give_back(a):
+        o = jnp.concatenate([acc[a, pr] / den[a, pr] for pr in range(pairs)], axis=1).astype(BF)
         for u in range(2):
-            dst = blk * 2 + u
+            dst = block_of(a) * 2 + u
             zout[dst] = o[u * step:u * step + cols]
 
             @pl.when(dst != me)
             def _():
                 zback(dst, me).start()
+
+    def zonal():
+        take_pieces(0, 4)
+
+        def near(a, _):
+            attend(a, 0, 2, True)
+            return 0
+
+        lax.fori_loop(0, 2, near, 0)
+        take_pieces(4, 2)
+        attend(2, 0, 3, True)
+
+        def far(a, _):
+            attend(a, 2, 1, False)
+            return 0
+
+        lax.fori_loop(0, 2, far, 0)
+        take_pieces(6, 2)
+
+        def last(t, _):
+            @pl.when(t == 1)
+            def _():
+                attend(3, 0, 4, True)
+
+            @pl.when(t != 1)
+            def _():
+                attend(a_of(t), 3, 1, False)
+
+            give_back(a_of(t))
+            return 0
+
+        def a_of(t):
+            return jnp.where(t == 0, 2, jnp.where(t == 1, 3, 3 - t))
+
+        lax.fori_loop(0, 4, last, 0)
+
+    gcols = group // lat_total
+    batch = batch_of(chunk // gcols)
+
+    def merid():
+        def more_merid(k, _):
+            a = lax.rem(la + k, nlat)
+            mcopy(la, a).wait_recv()
+            project_merid(colbuf[a], a)
+            return 0
+
+        lax.fori_loop(1, nlat, more_merid, 0)
+
+        def merid_batch(g, _):
+            for i in range(batch):
+                at = pl.ds((g * batch + i) * gcols, gcols)
+                for pr in range(pairs):
+                    w = slice(pr * 2 * HD, (pr + 1) * 2 * HD)
+                    q = jnp.concatenate(split_heads(mqkv[0, at, :, w].reshape(group, 2 * HD)), axis=0)
+                    k = mqkv[1, at, :, w].reshape(group, 2 * HD).astype(BF)
+                    ms_scr[i * pairs + pr] = mm_t(q, k) + mbias[pr]
+            for i in range(batch * pairs):
+                s = ms_scr[i]
+                e = jnp.exp2((s - jnp.max(s, axis=-1, keepdims=True)) * LOG2E)
+                mp_scr[i] = e.astype(BF)
+                ml_scr[i] = jnp.sum(e, axis=-1, keepdims=True)
+            keep = low(group)
+            for i in range(batch):
+                at = pl.ds((g * batch + i) * gcols, gcols)
+                outs = []
+                for pr in range(pairs):
+                    w = slice(pr * 2 * HD, (pr + 1) * 2 * HD)
+                    v = mqkv[2, at, :, w].reshape(group, 2 * HD).astype(BF)
+                    o = mm(mp_scr[i * pairs + pr], v) / ml_scr[i * pairs + pr]
+                    outs.append(jnp.where(keep, o[:group], o[group:]))
+                o = jnp.concatenate(outs, axis=1).reshape(gcols, lat_total, GW)
+                for a in range(nlat):
+                    mout[a, at] = o[:, a * rows:(a + 1) * rows, :].astype(BF)
+            return 0
+
+        lax.fori_loop(0, chunk // gcols // batch, merid_batch, 0)
+        for k in range(1, nlat):
+            mback(lax.rem(la + k, nlat), la).start()
+
+    project_merid(tok_ref[pl.ds(la * chunk, chunk)], la)
+
+    def half(i, _):
+        turn = lax.rem(i + odd, 2)
+
+        @pl.when(turn == 0)
+        def _():
+            zonal()
+
+        @pl.when(turn == 1)
+        def _():
+            merid()
+
         return 0
 
-    lax.fori_loop(0, nblk, zonal_block, 0)
+    lax.fori_loop(0, 2, half, 0)
+    mret[pl.ds(la * chunk, chunk)] = mout[la]
     zret[me] = zout[me]
 
     for k in range(1, nlat):
@@ -325,7 +421,8 @@
     out_ref[:, :, GW:2 * GW] = mret[...]
 
     def finish(i, _):
-        s = far_block(i // 2) * 2 + lax.rem(i, 2)
+        t = lax.rem(i, 4)
+        s = 2 * t + bit(lax.rem(t, 2), i // 4)
 
         @pl.when(s != me)
         def _():
@@ -362,6 +459,7 @@
     gcols = max(d for d in range(1, 128 // lat_total + 1) if chunk % d == 0)
     group = gcols * lat_total
     qb = 2 * step
+    nblk = nlon // 2
     vm = pl.BlockSpec(memory_space=pltpu.VMEM)
     sm = pl.BlockSpec(memory_space=pltpu.SMEM)
     dma = pltpu.SemaphoreType.DMA
@@ -376,14 +474,22 @@
             pltpu.VMEM((nlon, cols, width), BF),
             pltpu.VMEM((nlat, chunk, rows, width), BF),
             pltpu.VMEM((HALF, span, 2 * HD), BF),
-            pltpu.VMEM((HALF, 2 * span, 2 * HD), BF),
-            pltpu.VMEM((HALF, 2 * span, 2 * HD), BF),
+            pltpu.VMEM((HALF // 2, span, 2 * HD), BF),
+            pltpu.VMEM((HALF // 2, span, 2 * HD), BF),
             pltpu.VMEM((HALF, qb, span), F32),
-            pltpu.VMEM((HALF, group, group), F32),
+            pltpu.VMEM((HALF // 2, 2 * group, group), F32),
             pltpu.VMEM((3, chunk, lat_total, GW), F32),
             pltpu.VMEM((2, qb, span), F32),
             pltpu.VMEM((2, qb, span), BF),
             pltpu.VMEM((HALF, qb, 2 * HD), F32),
+            pltpu.VMEM((nblk, HALF, qb, 2 * HD), F32),
+            pltpu.VMEM((HALF, qb, 2 * HD), F32),
+            pltpu.VMEM((HALF, qb, 2 * HD), F32),
+            pltpu.VMEM((nblk, HALF // 2, qb, 2 * HD), F32),
+            pltpu.VMEM((nblk, HALF // 2, qb, 2 * HD), F32),
+            pltpu.VMEM((batch_of(chunk // gcols) * 2, 2 * group, group), F32),
+            pltpu.VMEM((batch_of(chunk // gcols) * 2, 2 * group, group), BF),
+            pltpu.VMEM((batch_of(chunk // gcols) * 2, 2 * group, 1), F32),
             pltpu.VMEM((nlon, cols, GW), BF),
             pltpu.VMEM((nlat, chunk, rows, GW), BF),
             pltpu.VMEM((nlon, cols, GW), BF),

time: 71.1 us -> 71.3 us (level)
  no operation moved by 1% of the time
where the time goes in v1:
time: 71.3 us; the launch traced here: 71.2 us
  Pallas kernels  67.8 us (95%)
  matrix products  3.41 us (5%)
    pallas_call x1, Pallas kernels, exchanged(): pl.pallas_call(functools.partial(kernel, (nlon, nlat, rows, cols, width))...  67.8 us
    dot_general x1, matrix products, mm(): return jnp.dot(a, b, preferred_element_type=F32)  3.41 us

profile of v1, /device:TPU:1, one launch (start us, length us, event | category | flops | bytes accessed | tf_op | source)
XLA Modules:
  0.0 71.2 jit_solution(14991204823080273263)
XLA Ops:
  0.0 0.0 copy-start
  0.0 67.8 %axial.1 = bf16[180,8,512]{2,1,0:T(8,128)(2,1)} custom-call(bf16[180,8,512]{2,1,0:T(8,128)(2,1)} %bitcast.12, f32[1,512]{1,0:T(1,128)} %bitcast.13, bf16[512,1536]{1,0:T(8,128)(2,1)} %wqkv_ref.1, f32[4]{0:T(128)} %zs_ref.1, f32[4]{0:T(128)} %ms_ref.1), custom_call_target="tpu_custom_call" | custom-call | tf_op jit(solution)/shard_map/axial/pallas_call | solution.py:466
  67.8 0.0 copy-done
  67.8 3.4 %fusion.1 = bf16[8,180,512]{2,0,1:T(8,128)(2,1)} fusion(bf16[512,512]{1,0:T(8,128)(2,1)S(1)} %copy-done, bf16[180,8,512]{2,1,0:T(8,128)(2,1)} %axial.1), kind=kOutput, calls=%fused_computation.2 | convolution fusion | flops 755712000 | bytes 3473408 | tf_op jit(solution)/shard_map/dot_general | solution.py:112
Async XLA Ops:
  0.0 67.8 %copy-start = (bf16[512,512]{1,0:T(8,128)(2,1)S(1)}, bf16[512,512]{1,0:T(8,128)(2,1)}, u32[]{:S(2)}) copy-start(bf16[512,512]{1,0:T(8,128)(2,1)} %param.9) | copy-start | bytes 1572868

commit v2 on v1

--- a/solution.py
+++ b/solution.py
@@ -194,7 +194,8 @@
 
     same = ((1, 1), (2, 0), (3, 1))
     other = ((0, 1), (1, 0), (2, 1), (3, 0))
-    for a, b in zip(same + other, other + same):
+    NEAR = ((0, 1), (1, 0), (1, 1), (2, 0), (2, 1), (3, 0), (3, 1))
+    for a, b in zip(NEAR, NEAR):
         r = (1 - odd) * peer(*a) + odd * peer(*b)
         take_row(r, rowsrc)
         zcopy(r, me).start()
@@ -400,7 +401,7 @@
     project_merid(tok_ref[pl.ds(la * chunk, chunk)], la)
 
     def half(i, _):
-        turn = lax.rem(i + odd, 2)
+        turn = lax.rem(i + 1, 2)
 
         @pl.when(turn == 0)
         def _():

time: 71.3 us -> 66.8 us (0.937)
  Pallas kernels: 67.8 us -> 63.2 us
    pallas_call x1, Pallas kernels: 67.8 us -> 63.2 us  [exchanged(): pl.pallas_call(functools.partial(kernel, (nlon, nlat, rows, cols, width))...]
where the time goes in v2:
time: 66.8 us; the launch traced here: 66.6 us
  Pallas kernels  63.2 us (95%)
  matrix products  3.41 us (5%)
    pallas_call x1, Pallas kernels, exchanged(): pl.pallas_call(functools.partial(kernel, (nlon, nlat, rows, cols, width))...  63.2 us
    dot_general x1, matrix products, mm(): return jnp.dot(a, b, preferred_element_type=F32)  3.41 us

profile of v2, /device:TPU:1, one launch (start us, length us, event | category | flops | bytes accessed | tf_op | source)
XLA Modules:
  0.0 66.6 jit_solution(9878322404207741670)
XLA Ops:
  0.0 0.0 copy-start
  0.0 63.2 %axial.1 = bf16[180,8,512]{2,1,0:T(8,128)(2,1)} custom-call(bf16[180,8,512]{2,1,0:T(8,128)(2,1)} %bitcast.12, f32[1,512]{1,0:T(1,128)} %bitcast.13, bf16[512,1536]{1,0:T(8,128)(2,1)} %wqkv_ref.1, f32[4]{0:T(128)} %zs_ref.1, f32[4]{0:T(128)} %ms_ref.1), custom_call_target="tpu_custom_call" | custom-call | tf_op jit(solution)/shard_map/axial/pallas_call | solution.py:467
  63.2 0.0 copy-done
  63.2 3.4 %fusion.1 = bf16[8,180,512]{2,0,1:T(8,128)(2,1)} fusion(bf16[512,512]{1,0:T(8,128)(2,1)S(1)} %copy-done, bf16[180,8,512]{2,1,0:T(8,128)(2,1)} %axial.1), kind=kOutput, calls=%fused_computation.2 | convolution fusion | flops 755712000 | bytes 3473408 | tf_op jit(solution)/shard_map/dot_general | solution.py:112
Async XLA Ops:
  0.0 63.2 %copy-start = (bf16[512,512]{1,0:T(8,128)(2,1)S(1)}, bf16[512,512]{1,0:T(8,128)(2,1)}, u32[]{:S(2)}) copy-start(bf16[512,512]{1,0:T(8,128)(2,1)} %param.9) | copy-start | bytes 1572868

commit v3 on v2

--- a/solution.py
+++ b/solution.py
@@ -320,7 +320,7 @@
             def _():
                 zback(dst, me).start()
 
-    def zonal():
+    def zonal_near():
         take_pieces(0, 4)
 
         def near(a, _):
@@ -328,6 +328,8 @@
             return 0
 
         lax.fori_loop(0, 2, near, 0)
+
+    def zonal_far():
         take_pieces(4, 2)
         attend(2, 0, 3, True)
 
@@ -400,20 +402,9 @@
 
     project_merid(tok_ref[pl.ds(la * chunk, chunk)], la)
 
-    def half(i, _):
-        turn = lax.rem(i + 1, 2)
-
-        @pl.when(turn == 0)
-        def _():
-            zonal()
-
-        @pl.when(turn == 1)
-        def _():
-            merid()
-
-        return 0
-
-    lax.fori_loop(0, 2, half, 0)
+    zonal_near()
+    merid()
+    zonal_far()
     mret[pl.ds(la * chunk, chunk)] = mout[la]
     zret[me] = zout[me]
 
@@ -422,8 +413,8 @@
     out_ref[:, :, GW:2 * GW] = mret[...]
 
     def finish(i, _):
-        t = lax.rem(i, 4)
-        s = 2 * t + bit(lax.rem(t, 2), i // 4)
+        t = i // 2
+        s = peer(jnp.where(t < 2, 2 + t, 3 - t), i % 2)
 
         @pl.when(s != me)
         def _():

time: 66.8 us -> 66 us (0.988)
  the two profiles are of different devices: /device:TPU:1 before, /device:TPU:14 now
where the time goes in v3:
time: 66 us; the launch traced here: 65.8 us
  Pallas kernels  62.4 us (95%)
  matrix products  3.42 us (5%)
    pallas_call x1, Pallas kernels, exchanged(): pl.pallas_call(functools.partial(kernel, (nlon, nlat, rows, cols, width))...  62.4 us
    dot_general x1, matrix products, mm(): return jnp.dot(a, b, preferred_element_type=F32)  3.42 us

profile of v3, /device:TPU:14, one launch (start us, length us, event | category | flops | bytes accessed | tf_op | source)
XLA Modules:
  0.0 65.8 jit_solution(8730141563673036337)
XLA Ops:
  0.0 0.0 copy-start
  0.0 62.4 %axial.1 = bf16[180,8,512]{2,1,0:T(8,128)(2,1)} custom-call(bf16[180,8,512]{2,1,0:T(8,128)(2,1)} %bitcast.12, f32[1,512]{1,0:T(1,128)} %bitcast.13, bf16[512,1536]{1,0:T(8,128)(2,1)} %wqkv_ref.1, f32[4]{0:T(128)} %zs_ref.1, f32[4]{0:T(128)} %ms_ref.1), custom_call_target="tpu_custom_call" | custom-call | tf_op jit(solution)/shard_map/axial/pallas_call | solution.py:458
  62.4 0.0 copy-done
  62.4 3.4 %fusion.1 = bf16[8,180,512]{2,0,1:T(8,128)(2,1)} fusion(bf16[512,512]{1,0:T(8,128)(2,1)S(1)} %copy-done, bf16[180,8,512]{2,1,0:T(8,128)(2,1)} %axial.1), kind=kOutput, calls=%fused_computation.2 | convolution fusion | flops 755712000 | bytes 3473408 | tf_op jit(solution)/shard_map/dot_general | solution.py:112
Async XLA Ops:
  0.0 62.4 %copy-start = (bf16[512,512]{1,0:T(8,128)(2,1)S(1)}, bf16[512,512]{1,0:T(8,128)(2,1)}, u32[]{:S(2)}) copy-start(bf16[512,512]{1,0:T(8,128)(2,1)} %param.9) | copy-start | bytes 1572868
